TPU v7x, 32 devices: a whole 2x2x4 slice. The times are simulated.
32 devices in a mesh: rep: 16 (over z, x, core), shard: 2 (over y).
Axes of the slice: x: 2, y: 2, z: 4, core: 2. Of those that a mesh axis runs over, the one named last changes fastest.
Arguments:
- images: bfloat16 [160, 197, 768], P(('rep', 'shard')), may hold values from -6 to 6
- ln1_gain: bfloat16 [768], P('shard'), may hold values from 0.25 to 1.75
- first_norm_bias: bfloat16 [768], P('shard'), may hold values from -3 to 3
- qkv_weight: bfloat16 [768, 2304], P('shard'), may hold values from -0.21875 to 0.21875
- q_bias: bfloat16 [768], P('shard'), may hold values from -3 to 3
- v_bias: bfloat16 [768], P('shard'), may hold values from -3 to 3
- out_weight: bfloat16 [768, 768], P('shard'), may hold values from -1.75 to 1.75
- out_bias: bfloat16 [768], P('shard'), may hold values from -3 to 3
- ln2_gain: bfloat16 [768], P('shard'), may hold values from 0.25 to 1.75
- second_norm_bias: bfloat16 [768], P('shard'), may hold values from -3 to 3
- up_weight: bfloat16 [768, 3072], P('shard'), may hold values from -0.21875 to 0.21875
- up_bias: bfloat16 [3072], P('shard'), may hold values from -3 to 3
- down_weight: bfloat16 [3072, 768], P('shard'), may hold values from -0.109375 to 0.109375
- down_bias: bfloat16 [768], P('shard'), may hold values from -3 to 3
- cotangent: bfloat16 [160, 197, 768], P(('rep', 'shard')), may hold values from -6 to 6
Outputs:
- result: bfloat16 [160, 197, 768], P(('rep', 'shard'))
- grad_images: bfloat16 [160, 197, 768], P(('rep', 'shard'))
- grad_ln1_gain: float32 [768], P('shard')
- grad_ln1_bias: float32 [768], P('shard')
- grad_qkv_weight: float32 [768, 2304], P('shard')
- grad_q_bias: float32 [768], P('shard')
- grad_v_bias: float32 [768], P('shard')
- grad_out_weight: float32 [768, 768], P('shard')
- grad_out_bias: float32 [768], P('shard')
- grad_ln2_gain: float32 [768], P('shard')
- grad_ln2_bias: float32 [768], P('shard')
- grad_up_weight: float32 [768, 3072], P('shard')
- grad_up_bias: float32 [3072], P('shard')
- grad_down_weight: float32 [3072, 768], P('shard')
- grad_down_bias: float32 [768], P('shard')
All inputs are finite; a program needn't handle non-finite values.
Results may differ from a plain program's by a relative error of at most 0.012.
Values may be sent and summed in bfloat16 or wider, within the bound.
No kernel may reach another device: no remote copies, remote signals or barrier semaphores. Data moves between devices by JAX's collectives and lax.ppermute only.
A program may use at most 256 MiB of HBM per device.

v0:
```python
import jax
import jax.numpy as jnp
from jax import lax
from jax.sharding import PartitionSpec as P

HEADS = 12


def matmul(left, right):
    return jnp.dot(left, right, preferred_element_type=jnp.float32)


def norm_statistics(token_rows):
    row_average = jnp.mean(token_rows, axis=-1, keepdims=True)
    centred = token_rows - row_average
    var = jnp.mean(centred * centred, axis=-1, keepdims=True)
    scale_factor = lax.rsqrt(var + 1e-06)
    return (centred * scale_factor, scale_factor)


def norm_backward(normalized_gradient, standardized_input, scale_factor, norm_gain):
    scaled_rows = normalized_gradient * norm_gain
    return scale_factor * (
        scaled_rows
        - jnp.mean(scaled_rows, axis=-1, keepdims=True)
        - standardized_input * jnp.mean(scaled_rows * standardized_input, axis=-1, keepdims=True)
    )


def gelu_parts(pre):
    cdf = 0.5 * (1.0 + lax.erf(pre * 0.7071067811865476))
    dens = jnp.exp(-0.5 * pre * pre) * 0.3989422804014327
    return (pre * cdf, cdf + pre * dens)


def per_device(
    images,
    ln1_gain,
    first_norm_bias,
    qkv_weight,
    q_bias,
    v_bias,
    out_weight,
    out_bias,
    ln2_gain,
    second_norm_bias,
    up_weight,
    up_bias,
    down_weight,
    down_bias,
    cotangent,
):
    count, seq, width = images.shape
    heads = HEADS
    head = width // heads
    scale = head ** (-0.5)
    single_float = jnp.float32
    brain_float16 = jnp.bfloat16
    attention_complete = (
        lax.all_gather(ln1_gain, "shard", axis=0, tiled=True),
        lax.all_gather(first_norm_bias, "shard", axis=0, tiled=True),
        lax.all_gather(qkv_weight, "shard", axis=0, tiled=True),
        lax.all_gather(q_bias, "shard", axis=0, tiled=True),
        lax.all_gather(v_bias, "shard", axis=0, tiled=True),
        lax.all_gather(out_weight, "shard", axis=0, tiled=True),
        lax.all_gather(out_bias, "shard", axis=0, tiled=True),
    )
    first_norm_gain = attention_complete[0].astype(single_float)
    token_rows = images.reshape(-1, width).astype(single_float)
    first_standardized, first_scale_factor = norm_statistics(token_rows)
    first_normalized = (
        first_standardized * first_norm_gain + attention_complete[1].astype(single_float)
    ).astype(brain_float16)
    bias_all = jnp.concatenate(
        [
            attention_complete[3].astype(single_float),
            jnp.zeros((width,), single_float),
            attention_complete[4].astype(single_float),
        ]
    )
    qkv = (matmul(first_normalized, attention_complete[2]) + bias_all).astype(brain_float16)
    query = qkv[:, :width].reshape(count, seq, heads, head)
    keys = qkv[:, width : 2 * width].reshape(count, seq, heads, head)
    values = qkv[:, 2 * width :].reshape(count, seq, heads, head)
    scores = jnp.einsum("nqhe,nkhe->nhqk", query, keys, preferred_element_type=single_float) * scale
    top = jnp.max(scores, axis=-1, keepdims=True)
    total = jnp.sum(jnp.exp(scores - top), axis=-1, keepdims=True)
    lse = top + jnp.log(total)
    prob_b = jnp.exp(scores - lse).astype(brain_float16)
    context = (
        jnp.einsum("nhqk,nkhe->nqhe", prob_b, values, preferred_element_type=single_float)
        .astype(brain_float16)
        .reshape(-1, width)
    )
    hidden_activation = (
        token_rows
        + matmul(context, attention_complete[5])
        + attention_complete[6].astype(single_float)
    )
    perceptron_complete = (
        lax.all_gather(ln2_gain, "shard", axis=0, tiled=True),
        lax.all_gather(second_norm_bias, "shard", axis=0, tiled=True),
        lax.all_gather(up_weight, "shard", axis=0, tiled=True),
        lax.all_gather(up_bias, "shard", axis=0, tiled=True),
        lax.all_gather(down_weight, "shard", axis=0, tiled=True),
        lax.all_gather(down_bias, "shard", axis=0, tiled=True),
    )
    second_norm_gain = perceptron_complete[0].astype(single_float)
    second_standardized, second_scale_factor = norm_statistics(hidden_activation)
    second_normalized = (
        second_standardized * second_norm_gain + perceptron_complete[1].astype(single_float)
    ).astype(brain_float16)
    pre = matmul(second_normalized, perceptron_complete[2]) + perceptron_complete[3].astype(
        single_float
    )
    act, slope = gelu_parts(pre)
    act_b = act.astype(brain_float16)
    result = (
        hidden_activation
        + matmul(act_b, perceptron_complete[4])
        + perceptron_complete[5].astype(single_float)
    ).astype(brain_float16)
    perceptron_backward = (
        lax.all_gather(ln2_gain, "shard", axis=0, tiled=True),
        lax.all_gather(second_norm_bias, "shard", axis=0, tiled=True),
        lax.all_gather(up_weight, "shard", axis=0, tiled=True),
        lax.all_gather(up_bias, "shard", axis=0, tiled=True),
        lax.all_gather(down_weight, "shard", axis=0, tiled=True),
        lax.all_gather(down_bias, "shard", axis=0, tiled=True),
    )
    cot = cotangent.reshape(-1, width)
    cotangent_float32 = cot.astype(single_float)
    g_down_bias = jnp.sum(cotangent_float32, axis=0)
    g_down = matmul(act_b.T, cot)
    dpre = matmul(cot, perceptron_backward[4].T) * slope
    dpre_b = dpre.astype(brain_float16)
    g_up_bias = jnp.sum(dpre, axis=0)
    g_up = matmul(second_normalized.T, dpre_b)
    second_normalized_gradient = matmul(dpre_b, perceptron_backward[2].T)
    second_norm_gain_gradient = jnp.sum(second_normalized_gradient * second_standardized, axis=0)
    g_ln2_bias = jnp.sum(second_normalized_gradient, axis=0)
    middle_gradient = cotangent_float32 + norm_backward(
        second_normalized_gradient,
        second_standardized,
        second_scale_factor,
        perceptron_backward[0].astype(single_float),
    )
    mlp_grads = (second_norm_gain_gradient, g_ln2_bias, g_up, g_up_bias, g_down, g_down_bias)
    mlp_pieces = (
        lax.psum_scatter(
            mlp_grads[0].astype(jnp.bfloat16), "shard", scatter_dimension=0, tiled=True
        ).astype(jnp.float32),
        lax.psum_scatter(
            mlp_grads[1].astype(jnp.bfloat16), "shard", scatter_dimension=0, tiled=True
        ).astype(jnp.float32),
        lax.psum_scatter(
            mlp_grads[2].astype(jnp.bfloat16), "shard", scatter_dimension=0, tiled=True
        ).astype(jnp.float32),
        lax.psum_scatter(
            mlp_grads[3].astype(jnp.bfloat16), "shard", scatter_dimension=0, tiled=True
        ).astype(jnp.float32),
        lax.psum_scatter(
            mlp_grads[4].astype(jnp.bfloat16), "shard", scatter_dimension=0, tiled=True
        ).astype(jnp.float32),
        lax.psum_scatter(
            mlp_grads[5].astype(jnp.bfloat16), "shard", scatter_dimension=0, tiled=True
        ).astype(jnp.float32),
    )
    p_ln2_gain, p_ln2_bias, p_up, p_up_bias, p_down, p_down_bias = mlp_pieces
    attention_backward = (
        lax.all_gather(ln1_gain, "shard", axis=0, tiled=True),
        lax.all_gather(first_norm_bias, "shard", axis=0, tiled=True),
        lax.all_gather(qkv_weight, "shard", axis=0, tiled=True),
        lax.all_gather(q_bias, "shard", axis=0, tiled=True),
        lax.all_gather(v_bias, "shard", axis=0, tiled=True),
        lax.all_gather(out_weight, "shard", axis=0, tiled=True),
        lax.all_gather(out_bias, "shard", axis=0, tiled=True),
    )
    dmiddle_b = middle_gradient.astype(brain_float16)
    g_out_bias = jnp.sum(middle_gradient, axis=0)
    g_out = matmul(context.T, dmiddle_b)
    dcontext = (
        matmul(dmiddle_b, attention_backward[5].T)
        .astype(brain_float16)
        .reshape(count, seq, heads, head)
    )
    again = jnp.einsum("nqhe,nkhe->nhqk", query, keys, preferred_element_type=single_float) * scale
    prob = jnp.exp(again - lse)
    prob_again = prob.astype(brain_float16)
    dprob = jnp.einsum("nqhe,nkhe->nhqk", dcontext, values, preferred_element_type=single_float)
    dvalue = jnp.einsum(
        "nhqk,nqhe->nkhe", prob_again, dcontext, preferred_element_type=single_float
    ).reshape(-1, width)
    delta = jnp.sum(prob * dprob, axis=-1, keepdims=True)
    dscore = (prob * (dprob - delta) * scale).astype(brain_float16)
    dquery = jnp.einsum(
        "nhqk,nkhe->nqhe", dscore, keys, preferred_element_type=single_float
    ).reshape(-1, width)
    dkey = jnp.einsum(
        "nhqk,nqhe->nkhe", dscore, query, preferred_element_type=single_float
    ).reshape(-1, width)
    g_q_bias = jnp.sum(dquery, axis=0)
    g_v_bias = jnp.sum(dvalue, axis=0)
    dqkv = jnp.concatenate([dquery, dkey, dvalue], axis=1).astype(brain_float16)
    g_qkv = matmul(first_normalized.T, dqkv)
    first_normalized_gradient = matmul(dqkv, attention_backward[2].T)
    first_norm_gain_gradient = jnp.sum(first_normalized_gradient * first_standardized, axis=0)
    g_ln1_bias = jnp.sum(first_normalized_gradient, axis=0)
    input_gradient = (
        middle_gradient
        + norm_backward(
            first_normalized_gradient,
            first_standardized,
            first_scale_factor,
            attention_backward[0].astype(single_float),
        )
    ).astype(brain_float16)
    attn_grads = (
        first_norm_gain_gradient,
        g_ln1_bias,
        g_qkv,
        g_q_bias,
        g_v_bias,
        g_out,
        g_out_bias,
    )
    attn_pieces = (
        lax.psum_scatter(
            attn_grads[0].astype(jnp.bfloat16), "shard", scatter_dimension=0, tiled=True
        ).astype(jnp.float32),
        lax.psum_scatter(
            attn_grads[1].astype(jnp.bfloat16), "shard", scatter_dimension=0, tiled=True
        ).astype(jnp.float32),
        lax.psum_scatter(
            attn_grads[2].astype(jnp.bfloat16), "shard", scatter_dimension=0, tiled=True
        ).astype(jnp.float32),
        lax.psum_scatter(
            attn_grads[3].astype(jnp.bfloat16), "shard", scatter_dimension=0, tiled=True
        ).astype(jnp.float32),
        lax.psum_scatter(
            attn_grads[4].astype(jnp.bfloat16), "shard", scatter_dimension=0, tiled=True
        ).astype(jnp.float32),
        lax.psum_scatter(
            attn_grads[5].astype(jnp.bfloat16), "shard", scatter_dimension=0, tiled=True
        ).astype(jnp.float32),
        lax.psum_scatter(
            attn_grads[6].astype(jnp.bfloat16), "shard", scatter_dimension=0, tiled=True
        ).astype(jnp.float32),
    )
    p_ln1_gain, p_ln1_bias, p_qkv, p_q_bias, p_v_bias, p_out, p_out_bias = attn_pieces
    (
        p_ln1_gain,
        p_ln1_bias,
        p_qkv,
        p_q_bias,
        p_v_bias,
        p_out,
        p_out_bias,
        p_ln2_gain,
        p_ln2_bias,
        p_up,
        p_up_bias,
        p_down,
        p_down_bias,
    ) = lax.psum(
        (
            p_ln1_gain,
            p_ln1_bias,
            p_qkv,
            p_q_bias,
            p_v_bias,
            p_out,
            p_out_bias,
            p_ln2_gain,
            p_ln2_bias,
            p_up,
            p_up_bias,
            p_down,
            p_down_bias,
        ),
        "rep",
    )
    return (
        result.reshape(count, seq, width),
        input_gradient.reshape(count, seq, width),
        p_ln1_gain,
        p_ln1_bias,
        p_qkv,
        p_q_bias,
        p_v_bias,
        p_out,
        p_out_bias,
        p_ln2_gain,
        p_ln2_bias,
        p_up,
        p_up_bias,
        p_down,
        p_down_bias,
    )


def solution(mesh):
    in_specs = (
        P(("rep", "shard"), None, None),
        P("shard"),
        P("shard"),
        P("shard", None),
        P("shard"),
        P("shard"),
        P("shard", None),
        P("shard"),
        P("shard"),
        P("shard"),
        P("shard", None),
        P("shard"),
        P("shard", None),
        P("shard"),
        P(("rep", "shard"), None, None),
    )
    out_specs = (
        P(("rep", "shard"), None, None),
        P(("rep", "shard"), None, None),
        P("shard"),
        P("shard"),
        P("shard", None),
        P("shard"),
        P("shard"),
        P("shard", None),
        P("shard"),
        P("shard"),
        P("shard"),
        P("shard", None),
        P("shard"),
        P("shard", None),
        P("shard"),
    )
    return jax.shard_map(
        per_device, mesh=mesh, in_specs=in_specs, out_specs=out_specs, check_vma=False
    )
```

profile of v0, /device:TPU:1, one launch (start us, length us, event | category | flops | bytes accessed | tf_op | source)
XLA Modules:
  0.0 828.6 jit_solution(5341018697626411092)
XLA Ops:
  47.8 13.3 %all-gather.14.cloned.1.call-done = bf16[768,2304]{1,0:T(8,128)(2,1)} async-done(((bf16[384,2304]{1,0:T(8,128)(2,1)}), bf16[768,2304]{1,0:T(8,128)(2,1)}) %all-gather.14.cloned.1.call-update) | async-done | bytes 3538960 | tf_op jit(solution)/shard_map/all_gather | solution.py:62
  61.1 6.3 add_convert_fusion
  68.8 5.8 reshape.201
  74.6 6.0 copy.66
  85.0 6.0 copy.65
  91.0 4.4 reshape.199
  95.4 5.5 copy.67
  115.1 4.6 reshape.154
  119.8 4.4 fusion.45
  126.4 23.3 %all-gather.18.cloned.1.call-done = bf16[768,3072]{1,0:T(8,128)(2,1)} async-done(((bf16[384,3072]{1,0:T(8,128)(2,1)}), bf16[768,3072]{1,0:T(8,128)(2,1)}) %all-gather.18.cloned.1.call-update) | async-done | bytes 4718608 | tf_op jit(solution)/shard_map/all_gather | solution.py:103
  149.7 13.7 %multiply_convert_fusion.1 = (bf16[985,3072]{1,0:T(8,128)(2,1)}, f32[985,3072]{1,0:T(8,128)}) fusion(f32[3072]{0:T(1024)S(1)} %bitcast.46, bf16[768,3072]{1,0:T(8,128)(2,1)} %all-gather.18.cloned.1.call-done, f32[985,768]{1,0:T(8,128)} %copy-done.5, f32[768]{0:T(1024)S(1)} %copy-done.25, f32[768]{0:T(1024)S(1)} %reshape.186, f32[985]{0:T(1024)S(1)} %add_rsqrt_fusion.1, ...), kind=kOutput, calls=%fused_computation.12 | convolution fusion | flops 4669751296 | bytes 25926344 | tf_op jit(solution)/shard_map/dot_general | solution.py:10
  163.3 50.4 %all-gather.20.cloned.1.call-done = bf16[3072,768]{1,0:T(8,128)(2,1)} async-done(((bf16[1536,768]{1,0:T(8,128)(2,1)}), bf16[3072,768]{1,0:T(8,128)(2,1)}) %all-gather.20.cloned.1.call-update) | async-done | bytes 4718608 | tf_op jit(solution)/shard_map/all_gather | solution.py:105
  213.7 11.6 %fusion.48 = (bf16[3072]{0:T(1024)(128)(2,1)S(1)}, bf16[985,3072]{1,0:T(8,128)(2,1)S(1)}) fusion(f32[985,3072]{1,0:T(8,128)} %get-tuple-element.55, f32[3072]{0:T(1024)S(1)} %bitcast.47, bf16[985,768]{1,0:T(8,128)(2,1)S(1)} %copy-done.15, bf16[3072,768]{1,0:T(8,128)(2,1)} %all-gather.20.cloned.1.call-done), kind=kOutput, calls=%fused_computation.97 | convolution fusion | flops 4684121088 | bytes 24405504 | tf_op jit(solution)/shard_map/dot_general | solution.py:10
  225.3 5.5 multiply_reduce_fusion.3
  239.9 4.4 reshape.202
  244.3 6.2 copy.71
  250.5 9.5 %bitcast_convert_fusion = (bf16[5,197,12,64]{1,3,2,0:T(8,128)(2,1)S(1)}, f32[5,12,64,197]{3,2,1,0:T(8,128)}) fusion(bf16[5,197,12,64]{1,3,2,0:T(8,128)(2,1)} %copy.71, f32[5,12,197,197]{2,3,1,0:T(8,128)} %copy-done, f32[5,12,197]{2,1,0:T(8,128)S(1)} %copy-done.20), kind=kOutput, calls=%fused_computation.27 | convolution fusion | flops 305795232 | bytes 15413280 | tf_op jit(solution)/shard_map/nhqk,nqhe->nkhe/dot_general | solution.py:191
  260.0 6.2 fusion.49
  269.4 5.7 reshape.160
  275.1 20.7 %bitcast_convert_fusion.1 = (bf16[5,197,12,64]{1,3,2,0:T(8,128)(2,1)}, f32[5,12,64,197]{3,2,1,0:T(8,128)}) fusion(bf16[5,197,12,64]{1,3,2,0:T(8,128)(2,1)S(1)} %copy-done.4, f32[5,12,197,197]{2,3,1,0:T(8,128)} %fusion.49, f32[5,12,197,197]{2,3,1,0:T(8,128)} %copy-done, f32[5,12,197]{2,1,0:T(8,128)S(1)} %copy-done.20), kind=kOutput, calls=%fused_computation.29 | convolution fusion | flops 319778464 | bytes 24727440 | tf_op jit(solution)/shard_map/nhqk,nkhe->nqhe/dot_general | solution.py:196
  295.8 4.7 copy.75
  300.4 6.1 reshape.158
  306.6 19.3 %convert_bitcast_fusion = bf16[5,197,12,64]{1,3,2,0:T(8,128)(2,1)} fusion(bf16[5,197,12,64]{1,3,2,0:T(8,128)(2,1)S(1)} %copy-done.3, f32[5,12,197,197]{2,3,1,0:T(8,128)} %fusion.49, f32[5,12,197,197]{2,3,1,0:T(8,128)} %copy-done, f32[5,12,197]{2,1,0:T(8,128)S(1)} %copy-done.20), kind=kOutput, calls=%fused_computation.49 | convolution fusion | flops 319778464 | bytes 21701520 | tf_op jit(solution)/shard_map/nhqk,nqhe->nkhe/dot_general | solution.py:199
  337.1 6.1 convolution_convert_fusion.2
  344.5 9.7 %convolution_convert_fusion = bf16[3072,768]{1,0:T(8,128)(2,1)} fusion(bf16[985,3072]{1,0:T(8,128)(2,1)} %get-tuple-element.54, bf16[985,768]{1,0:T(8,128)(2,1)S(1)} %copy-done.16), kind=kOutput, calls=%fused_computation.23 | convolution fusion | flops 4650172416 | bytes 12283392 | tf_op jit(solution)/shard_map/dot_general | solution.py:10
  356.1 9.8 %convolution_convert_fusion.1 = bf16[768,3072]{1,0:T(8,128)(2,1)} fusion(bf16[985,3072]{1,0:T(8,128)(2,1)} %copy-done.37, f32[985,768]{1,0:T(8,128)S(1)} %copy-done.7, f32[768]{0:T(1024)S(1)} %copy-done.25, f32[768]{0:T(1024)S(1)} %reshape.186, f32[985]{0:T(1024)S(1)} %add_rsqrt_fusion.1, f32[985]{0:T(1024)S(1)} %broadcast_multiply_fusion.5), kind=kOutput, calls=%fused_computation.24 | convolution fusion | flops 4653955072 | bytes 13810376 | tf_op jit(solution)/shard_map/dot_general | solution.py:10
  374.0 10.1 %add_convert_fusion.2 = bf16[985,768]{1,0:T(8,128)(2,1)} fusion(f32[985,768]{1,0:T(8,128)S(1)} %copy-done.7, bf16[985,3072]{1,0:T(8,128)(2,1)} %get-tuple-element.54, bf16[3072,768]{1,0:T(8,128)(2,1)} %all-gather.20.cloned.1.call-done, f32[768]{0:T(1024)S(1)} %reshape.189), kind=kOutput, calls=%fused_computation.40 | convolution fusion | flops 4650083328 | bytes 15312384 | tf_op jit(solution)/shard_map/dot_general | solution.py:10
  392.3 8.6 %multiply_reduce_fusion.4 = (bf16[768]{0:T(1024)(128)(2,1)S(1)}, f32[985]{0:T(1024)S(1)}, f32[985]{0:T(1024)S(1)}, bf16[768]{0:T(1024)(128)(2,1)S(1)}, f32[985,768]{1,0:T(8,128)S(1)}) fusion(f32[985,768]{1,0:T(8,128)S(1)} %copy-done.12, f32[985]{0:T(1024)S(1)} %rsqrt.20, f32[985]{0:T(1024)S(1)} %div.27, f32[768]{0:T(1024)S(1)} %reshape.181, ...), kind=kOutput, calls=%fused_computation.32 | convolution fusion | flops 3492664576 | bytes 14151568 | tf_op jit(solution)/shard_map/dot_general | solution.py:10
  406.0 6.8 all-reduce.10
  413.5 40.4 %reduce-scatter.11.cloned.1.call-done = bf16[1536,768]{1,0:T(8,128)(2,1)} async-done(((bf16[3072,768]{1,0:T(8,128)(2,1)}), bf16[1536,768]{1,0:T(8,128)(2,1)}) %reduce-scatter.11.cloned.1.call-update) | async-done | bytes 2359312 | tf_op jit(solution)/shard_map/reduce_scatter | solution.py:162
  453.9 63.0 %reduce-scatter.9.cloned.1.call-done = bf16[384,3072]{1,0:T(8,128)(2,1)} async-done(((bf16[768,3072]{1,0:T(8,128)(2,1)}), bf16[384,3072]{1,0:T(8,128)(2,1)}) %reduce-scatter.9.cloned.1.call-update) | async-done | bytes 2359312 | tf_op jit(solution)/shard_map/reduce_scatter | solution.py:156
  516.9 304.7 %all-reduce.12 = (f32[384]{0:T(512)}, f32[384]{0:T(512)}, f32[384,2304]{1,0:T(8,128)}, f32[384]{0:T(512)}, f32[384]{0:T(512)}, /*index=5*/f32[384,768]{1,0:T(8,1...) all-reduce(f32[384]{0:T(512)S(1)} %dynamic-slice_convert_fusion.8, ...), channel_id=1, replica_groups=mesh['rep'=16,'shard'=2] {'rep'}, use_global_device_ids=true, to_apply=%region_13.0 | all-reduce | flops 3543552 | bytes 21270528 | tf_op jit(solution)/shard_map/psum | solution.py:265
  (180 shorter events, 109.7 us)
Async XLA Ops:
  7.2 53.9 %all-gather.14.cloned.1.call-start = ((), (), s32[]{:S(2)}) async-start(), calls=%async_computation.4 | async-start | bytes 5308416 | tf_op jit(solution)/shard_map/all_gather | solution.py:62
  7.9 111.9 %all-gather.16.cloned.1.call-start = ((), (), s32[]{:S(2)}) async-start(), calls=%async_computation.5 | async-start | bytes 1769472 | tf_op jit(solution)/shard_map/all_gather | solution.py:65
  8.7 141.0 %all-gather.18.cloned.1.call-start = ((), (), s32[]{:S(2)}) async-start(), calls=%async_computation.6 | async-start | bytes 7077888 | tf_op jit(solution)/shard_map/all_gather | solution.py:103
  9.4 204.3 %all-gather.20.cloned.1.call-start = ((), (), s32[]{:S(2)}) async-start(), calls=%async_computation.7 | async-start | bytes 7077888 | tf_op jit(solution)/shard_map/all_gather | solution.py:105
  10.0 403.6 %reduce-scatter.7.cloned.1.call-start = ((), (), s32[]{:S(2)}) async-start(), calls=%async_computation.9 | async-start | bytes 1769472 | tf_op jit(solution)/shard_map/reduce_scatter | solution.py:243
  10.4 6.7 copy-start.28
  10.4 9.9 %copy-start.29 = (bf16[384]{0:T(512)(128)(2,1)S(1)}, bf16[384]{0:T(512)(128)(2,1)}, u32[]{:S(2)}) copy-start(bf16[384]{0:T(512)(128)(2,1)} %param.19) | copy-start | bytes 2308
  10.4 13.5 %copy-start.30 = (bf16[384]{0:T(512)(128)(2,1)S(1)}, bf16[384]{0:T(512)(128)(2,1)}, u32[]{:S(2)}) copy-start(bf16[384]{0:T(512)(128)(2,1)} %param.20) | copy-start | bytes 2308
  10.5 17.4 %copy-start.31 = (bf16[384]{0:T(512)(128)(2,1)S(1)}, bf16[384]{0:T(512)(128)(2,1)}, u32[]{:S(2)}) copy-start(bf16[384]{0:T(512)(128)(2,1)} %param.22) | copy-start | bytes 2308
  10.5 21.7 %copy-start.32 = (bf16[384]{0:T(512)(128)(2,1)S(1)}, bf16[384]{0:T(512)(128)(2,1)}, u32[]{:S(2)}) copy-start(bf16[384]{0:T(512)(128)(2,1)} %param.23) | copy-start | bytes 2308
  10.5 25.4 %copy-start.33 = (bf16[384]{0:T(512)(128)(2,1)S(1)}, bf16[384]{0:T(512)(128)(2,1)}, u32[]{:S(2)}) copy-start(bf16[384]{0:T(512)(128)(2,1)} %param.24) | copy-start | bytes 2308
  10.5 29.7 %copy-start.26 = (bf16[1536]{0:T(1024)(128)(2,1)S(1)}, bf16[1536]{0:T(1024)(128)(2,1)}, u32[]{:S(2)}) copy-start(bf16[1536]{0:T(1024)(128)(2,1)} %param.26) | copy-start | bytes 9220
  13.1 48.0 %copy-start.10 = (f32[985,768]{1,0:T(8,128)S(1)}, f32[985,768]{1,0:T(8,128)}, u32[]{:S(2)}) copy-start(f32[985,768]{1,0:T(8,128)} %reshape.162) | copy-start | bytes 9077764
  20.3 47.1 %copy-start.23 = (f32[768]{0:T(1024)}, f32[768]{0:T(1024)S(1)}, u32[]{:S(2)}) copy-start(f32[768]{0:T(1024)S(1)} %reshape.182) | copy-start | bytes 9220
  105.0 4.5 copy-start
  119.8 4.4 copy-start.17
  124.2 25.4 %copy-start.22 = (f32[2,1,1536]{2,1,0:T(1,128)S(1)}, f32[2,1,1536]{2,1,0:T(1,128)}, u32[]{:S(2)}) copy-start(f32[2,1,1536]{2,1,0:T(1,128)} %convert_element_type.226) | copy-start | bytes 36868
  124.2 25.4 %copy-start.25 = (f32[768]{0:T(1024)S(1)}, f32[768]{0:T(1024)}, u32[]{:S(2)}) copy-start(f32[768]{0:T(1024)} %reshape.187) | copy-start | bytes 9220
  149.7 64.1 %copy-start.15 = (bf16[985,768]{1,0:T(8,128)(2,1)S(1)}, bf16[985,768]{1,0:T(8,128)(2,1)}, u32[]{:S(2)}) copy-start(bf16[985,768]{1,0:T(8,128)(2,1)} %reshape.156) | copy-start | bytes 4538884
  213.7 11.6 %copy-start.6 = (f32[985,768]{1,0:T(8,128)S(1)}, f32[985,768]{1,0:T(8,128)}, u32[]{:S(2)}) copy-start(f32[985,768]{1,0:T(8,128)} %copy-done.5) | copy-start | bytes 9077764
  213.7 11.6 %copy-start.35 = (bf16[768,3072]{1,0:T(8,128)(2,1)S(1)}, bf16[768,3072]{1,0:T(8,128)(2,1)}, u32[]{:S(2)}) copy-start(bf16[768,3072]{1,0:T(8,128)(2,1)} %all-gather.18.cloned.1.call-done) | copy-start | bytes 14155780
  225.3 5.5 copy-start.37
  230.9 3.0 copy-start.18
  236.3 177.3 %reduce-scatter.5.cloned.1.call-start = ((), (), s32[]{:S(2)}) async-start(), calls=%async_computation.8 | async-start | bytes 5308416 | tf_op jit(solution)/shard_map/reduce_scatter | solution.py:234
  244.3 6.2 copy-start.20
  250.5 9.5 %copy-start.1 = (bf16[5,197,12,64]{1,3,2,0:T(8,128)(2,1)S(1)}, bf16[5,197,12,64]{1,3,2,0:T(8,128)(2,1)}, u32[]{:S(2)}) copy-start(bf16[5,197,12,64]{1,3,2,0:T(8,128)(2,1)} %copy.71) | copy-start | bytes 4538884
  269.4 5.7 copy-start.4
  300.4 6.1 copy-start.3
  343.1 110.8 %reduce-scatter.11.cloned.1.call-start = ((), (), s32[]{:S(2)}) async-start(), calls=%async_computation.11 | async-start | bytes 7077888 | tf_op jit(solution)/shard_map/reduce_scatter | solution.py:162
  354.2 162.7 %reduce-scatter.9.cloned.1.call-start = ((), (), s32[]{:S(2)}) async-start(), calls=%async_computation.10 | async-start | bytes 7077888 | tf_op jit(solution)/shard_map/reduce_scatter | solution.py:156
  387.0 5.3 copy-start.12
  392.3 8.7 %copy-start.9 = (f32[985,768]{1,0:T(8,128)S(1)}, f32[985,768]{1,0:T(8,128)}, u32[]{:S(2)}) copy-start(f32[985,768]{1,0:T(8,128)} %copy-done.8) | copy-start | bytes 9077764
  (14 other events, 29.0 us)
Sparse Core Ops, SparseCore 0:
  9.5 51.5 all-gather.13
  62.6 22.7 all-gather.15
  87.0 62.6 all-gather.17
  151.1 62.6 all-gather.19
  236.4 21.8 reduce-scatter.6
  343.2 47.7 reduce-scatter.4
  393.3 60.5 reduce-scatter.10
  456.8 60.0 reduce-scatter.8
where the time goes:
time: 832 us; the launch traced here: 829 us
  blocking collectives  345 us (41%)
  waiting for transfers between devices  193 us (23%)
  matrix products  154 us (19%)
  local copies, waits for them, and re-layouts  104 us (12%)
  between operations  16.2 us (2%)
  other arithmetic  16 us (2%)
    psum x1, blocking collectives, per_device(): lax.psum((p_ln1_gain, p_ln1_bias, p_qkv, p_q_bias, p_v_bias, p_out, p_out...  305 us
    dot_general x12, matrix products, matmul(): return jnp.dot(left, right, preferred_element_type=jnp.float32)  91.7 us
    reduce_scatter x1, waiting for transfers between devices, per_device(): lax.psum_scatter(mlp_grads[2].astype(jnp.bfloat16), 'shard', scatter_dime...  63 us
    all_gather x1, waiting for transfers between devices, per_device(): lax.all_gather(down_weight, 'shard', axis=0, tiled=True)  50.4 us
    reduce_scatter x1, waiting for transfers between devices, per_device(): lax.psum_scatter(mlp_grads[4].astype(jnp.bfloat16), 'shard', scatter_dime...  40.4 us
    all_gather x1, waiting for transfers between devices, per_device(): lax.all_gather(up_weight, 'shard', axis=0, tiled=True)  23.3 us
    dot_general x1, matrix products, per_device(): jnp.einsum('nhqk,nkhe->nqhe', dscore, keys, preferred_element_type=single...  20.7 us
    dot_general x1, matrix products, per_device(): jnp.einsum('nhqk,nqhe->nkhe', dscore, query, preferred_element_type=singl...  19.3 us
  transfers between devices with their start and end apart: 8, of which 5 were waited for; matrix products, arithmetic and copies ran while one was open for 29% of the time, Pallas kernels for 0%

commit v1 on v0

--- a/solution.py
+++ b/solution.py
@@ -2,8 +2,31 @@
 import jax.numpy as jnp
 from jax import lax
 from jax.sharding import PartitionSpec as P
+from jax.lax import axis_index, axis_size, ppermute
 
 HEADS = 12
+
+
+def guide_block(x_in, in_dim):
+    far_arr = list(x_in.shape[1:])
+    far_arr[in_dim] *= x_in.shape[0]
+    back = jnp.moveaxis(x_in, 0, in_dim).reshape(far_arr)
+    return back
+
+
+def convert_the_halves(patch, link_axis):
+    shares = axis_size(link_axis)
+    oldest = patch[None]
+    for q in range(shares.bit_length() - 1):
+        later = 1 << q
+        buffer = []
+        for tick in tuple(range(shares)):
+            buffer.append((tick, tick ^ later))
+        long_array = ppermute(oldest, link_axis, buffer)
+        odd = jnp.stack([oldest, long_array], 0)
+        built = axis_index(link_axis) >> q & 1
+        oldest = jnp.where(built == 0, odd, odd[::-1]).reshape(-1, *patch.shape)
+    return oldest
 
 
 def matmul(left, right):
@@ -97,12 +120,18 @@
         + matmul(context, attention_complete[5])
         + attention_complete[6].astype(single_float)
     )
+
+    def change_sheets(buf, local_array, axis_no):
+        local_now = convert_the_halves(buf, local_array)
+        before = guide_block(local_now, axis_no)
+        return before
+
     perceptron_complete = (
         lax.all_gather(ln2_gain, "shard", axis=0, tiled=True),
         lax.all_gather(second_norm_bias, "shard", axis=0, tiled=True),
         lax.all_gather(up_weight, "shard", axis=0, tiled=True),
         lax.all_gather(up_bias, "shard", axis=0, tiled=True),
-        lax.all_gather(down_weight, "shard", axis=0, tiled=True),
+        change_sheets(down_weight, "shard", 0),
         lax.all_gather(down_bias, "shard", axis=0, tiled=True),
     )
     second_norm_gain = perceptron_complete[0].astype(single_float)

time: 832 us -> 873 us (1.049)
  blocking collectives: 345 us -> 427 us
  waiting for transfers between devices: 193 us -> 146 us
    all_gather x1, blocking collectives: 3.85 us -> 87.6 us  [per_device(): lax.all_gather(down_bias, 'shard', axis=0, tiled=True)]
    reduce_scatter x1, waiting for transfers between devices: 63 us -> 0.01 us  [per_device(): lax.psum_scatter(mlp_grads[2].astype(jnp.bfloat16), 'shard', scatter_dime...]
    reduce_scatter x1, waiting for transfers between devices: 40.4 us -> 55.9 us  [per_device(): lax.psum_scatter(mlp_grads[4].astype(jnp.bfloat16), 'shard', scatter_dime...]
  transfers between devices with their start and end apart: 8 -> 9, of which waited for: 5 -> 4; matrix products, arithmetic and copies ran while one was open for 29% -> 26% of each run, Pallas kernels for 0% -> 0%
where the time goes in v1:
time: 873 us; the launch traced here: 869 us
  blocking collectives  427 us (49%)
  matrix products  157 us (18%)
  waiting for transfers between devices  146 us (17%)
  local copies, waits for them, and re-layouts  102 us (12%)
  other arithmetic  20.1 us (2%)
  between operations  16.5 us (2%)
    psum x1, blocking collectives, per_device(): lax.psum((p_ln1_gain, p_ln1_bias, p_qkv, p_q_bias, p_v_bias, p_out, p_out...  305 us
    dot_general x12, matrix products, matmul(): return jnp.dot(left, right, preferred_element_type=jnp.float32)  92.3 us
    all_gather x1, blocking collectives, per_device(): lax.all_gather(down_bias, 'shard', axis=0, tiled=True)  87.6 us
    reduce_scatter x1, waiting for transfers between devices, per_device(): lax.psum_scatter(mlp_grads[4].astype(jnp.bfloat16), 'shard', scatter_dime...  55.9 us
    all_gather x1, waiting for transfers between devices, per_device(): lax.all_gather(down_weight, 'shard', axis=0, tiled=True)  50.6 us
    all_gather x1, waiting for transfers between devices, per_device(): lax.all_gather(up_weight, 'shard', axis=0, tiled=True)  23.4 us
    dot_general x1, matrix products, per_device(): jnp.einsum('nhqk,nkhe->nqhe', dscore, keys, preferred_element_type=single...  20.7 us
    dot_general x1, matrix products, per_device(): jnp.einsum('nhqk,nqhe->nkhe', dscore, query, preferred_element_type=singl...  19.4 us
  transfers between devices with their start and end apart: 9, of which 4 were waited for; matrix products, arithmetic and copies ran while one was open for 26% of the time, Pallas kernels for 0%

profile of v1, /device:TPU:1, one launch (start us, length us, event | category | flops | bytes accessed | tf_op | source)
XLA Modules:
  0.0 868.8 jit_solution(13663687220415570600)
XLA Ops:
  48.1 13.0 %all-gather.14.cloned.1.call-done = bf16[768,2304]{1,0:T(8,128)(2,1)} async-done(((bf16[384,2304]{1,0:T(8,128)(2,1)}), bf16[768,2304]{1,0:T(8,128)(2,1)}) %all-gather.14.cloned.1.call-update) | async-done | bytes 3538960 | tf_op jit(solution)/shard_map/all_gather | solution.py:85
  61.1 6.3 add_convert_fusion
  68.8 5.8 reshape.200
  74.6 6.0 copy.65
  85.0 6.0 copy.66
  91.0 4.4 reshape.199
  95.4 5.4 copy.67
  115.1 4.6 reshape.154
  119.8 4.4 fusion.45
  126.3 23.4 %all-gather.18.cloned.1.call-done = bf16[768,3072]{1,0:T(8,128)(2,1)} async-done(((bf16[384,3072]{1,0:T(8,128)(2,1)}), bf16[768,3072]{1,0:T(8,128)(2,1)}) %all-gather.18.cloned.1.call-update) | async-done | bytes 4718608 | tf_op jit(solution)/shard_map/all_gather | solution.py:132
  149.7 13.4 %multiply_convert_fusion.1 = (bf16[985,3072]{1,0:T(8,128)(2,1)}, f32[985,3072]{1,0:T(8,128)}) fusion(f32[3072]{0:T(1024)S(1)} %bitcast.53, bf16[768,3072]{1,0:T(8,128)(2,1)} %all-gather.18.cloned.1.call-done, f32[985,768]{1,0:T(8,128)} %copy-done.5, f32[768]{0:T(1024)S(1)} %copy-done.25, f32[768]{0:T(1024)S(1)} %reshape.186, f32[985]{0:T(1024)S(1)} %add_rsqrt_fusion.1, ...), kind=kOutput, calls=%fused_computation.12 | convolution fusion | flops 4669751296 | bytes 25926344 | tf_op jit(solution)/shard_map/dot_general | solution.py:33
  163.1 50.6 %all-gather.20.cloned.1.call-done = bf16[3072,768]{1,0:T(8,128)(2,1)} async-done(((bf16[1536,768]{1,0:T(8,128)(2,1)}), bf16[3072,768]{1,0:T(8,128)(2,1)}) %all-gather.20.cloned.1.call-update) | async-done | bytes 4718608 | tf_op jit(solution)/shard_map/all_gather | solution.py:157
  213.7 11.6 %fusion.48 = (bf16[3072]{0:T(1024)(128)(2,1)S(1)}, bf16[985,3072]{1,0:T(8,128)(2,1)S(1)}) fusion(f32[985,3072]{1,0:T(8,128)} %get-tuple-element.55, f32[3072]{0:T(1024)S(1)} %bitcast.54, bf16[985,768]{1,0:T(8,128)(2,1)S(1)} %copy-done.16, bf16[3072,768]{1,0:T(8,128)(2,1)} %all-gather.20.cloned.1.call-done), kind=kOutput, calls=%fused_computation.99 | convolution fusion | flops 4684121088 | bytes 24405504 | tf_op jit(solution)/shard_map/dot_general | solution.py:33
  225.3 5.5 multiply_reduce_fusion.3
  240.3 4.4 reshape.202
  244.6 6.1 copy.71
  250.7 10.0 %bitcast_convert_fusion = (bf16[5,197,12,64]{1,3,2,0:T(8,128)(2,1)}, f32[5,12,64,197]{3,2,1,0:T(8,128)}) fusion(bf16[5,197,12,64]{1,3,2,0:T(8,128)(2,1)} %copy.71, f32[5,12,197,197]{2,3,1,0:T(8,128)} %copy-done, f32[5,12,197]{2,1,0:T(8,128)S(1)} %copy-done.20), kind=kOutput, calls=%fused_computation.29 | convolution fusion | flops 305795232 | bytes 15413280 | tf_op jit(solution)/shard_map/nhqk,nqhe->nkhe/dot_general | solution.py:220
  260.8 8.0 fusion.49
  271.9 5.8 reshape.160
  277.7 19.4 %convert_bitcast_fusion = bf16[5,197,12,64]{1,3,2,0:T(8,128)(2,1)} fusion(bf16[5,197,12,64]{1,3,2,0:T(8,128)(2,1)S(1)} %copy-done.4, f32[5,12,197,197]{2,3,1,0:T(8,128)} %fusion.49, f32[5,12,197,197]{2,3,1,0:T(8,128)} %copy-done, f32[5,12,197]{2,1,0:T(8,128)S(1)} %copy-done.20), kind=kOutput, calls=%fused_computation.51 | convolution fusion | flops 319778464 | bytes 21701520 | tf_op jit(solution)/shard_map/nhqk,nqhe->nkhe/dot_general | solution.py:228
  297.2 4.7 copy.78
  301.8 5.7 reshape.159
  307.5 20.7 %bitcast_convert_fusion.1 = (bf16[5,197,12,64]{1,3,2,0:T(8,128)(2,1)}, f32[5,12,64,197]{3,2,1,0:T(8,128)}) fusion(bf16[5,197,12,64]{1,3,2,0:T(8,128)(2,1)S(1)} %copy-done.3, f32[5,12,197,197]{2,3,1,0:T(8,128)} %fusion.49, f32[5,12,197,197]{2,3,1,0:T(8,128)} %copy-done, f32[5,12,197]{2,1,0:T(8,128)S(1)} %copy-done.20), kind=kOutput, calls=%fused_computation.31 | convolution fusion | flops 319778464 | bytes 24727440 | tf_op jit(solution)/shard_map/nhqk,nkhe->nqhe/dot_general | solution.py:225
  339.4 6.3 convolution_convert_fusion.2
  347.5 9.8 %convolution_convert_fusion.1 = bf16[768,3072]{1,0:T(8,128)(2,1)} fusion(bf16[985,3072]{1,0:T(8,128)(2,1)} %copy-done.37, f32[985,768]{1,0:T(8,128)S(1)} %copy-done.7, f32[768]{0:T(1024)S(1)} %copy-done.25, f32[768]{0:T(1024)S(1)} %reshape.186, f32[985]{0:T(1024)S(1)} %add_rsqrt_fusion.1, f32[985]{0:T(1024)S(1)} %broadcast_multiply_fusion.5), kind=kOutput, calls=%fused_computation.25 | convolution fusion | flops 4653955072 | bytes 13810376 | tf_op jit(solution)/shard_map/dot_general | solution.py:33
  357.3 9.1 %convolution_convert_fusion = bf16[3072,768]{1,0:T(8,128)(2,1)} fusion(bf16[985,3072]{1,0:T(8,128)(2,1)} %get-tuple-element.54, bf16[985,768]{1,0:T(8,128)(2,1)} %reshape.156), kind=kOutput, calls=%fused_computation.24 | convolution fusion | flops 4650172416 | bytes 12283392 | tf_op jit(solution)/shard_map/dot_general | solution.py:33
  370.4 87.6 %all-gather.8 = bf16[2,1,384]{2,1,0:T(2,128)(2,1)S(1)} all-gather(bf16[1,1,384]{2,1,0:T(2,128)(2,1)S(1)} %reshape.179), channel_id=1, replica_groups=mesh['rep'=16,'shard'=2] {'shard'}, dimensions={0}, use_global_device_ids=true | all-gather | bytes 2304 | tf_op jit(solution)/shard_map/all_gather | solution.py:135
  466.8 9.8 %multiply_reduce_fusion.4 = (bf16[768]{0:T(1024)(128)(2,1)S(1)}, f32[985]{0:T(1024)S(1)}, f32[985]{0:T(1024)S(1)}, bf16[768]{0:T(1024)(128)(2,1)S(1)}, f32[985,768]{1,0:T(8,128)S(1)}) fusion(f32[985,768]{1,0:T(8,128)} %reshape.162, f32[985]{0:T(1024)S(1)} %rsqrt.20, f32[985]{0:T(1024)S(1)} %div.27, f32[768]{0:T(1024)S(1)} %reshape.181, ...), kind=kOutput, calls=%fused_computation.34 | convolution fusion | flops 3492664576 | bytes 14151568 | tf_op jit(solution)/shard_map/dot_general | solution.py:33
  481.9 10.1 %add_convert_fusion.2 = bf16[985,768]{1,0:T(8,128)(2,1)} fusion(f32[985,768]{1,0:T(8,128)S(1)} %copy-done.7, bf16[985,3072]{1,0:T(8,128)(2,1)} %get-tuple-element.54, bf16[3072,768]{1,0:T(8,128)(2,1)} %bitcast.52, f32[768]{0:T(1024)S(1)} %reshape.189), kind=kOutput, calls=%fused_computation.42 | convolution fusion | flops 4650083328 | bytes 15312384 | tf_op jit(solution)/shard_map/dot_general | solution.py:33
  494.9 5.2 all-reduce.10
  500.9 55.9 %reduce-scatter.11.cloned.1.call-done = bf16[1536,768]{1,0:T(8,128)(2,1)} async-done(((bf16[3072,768]{1,0:T(8,128)(2,1)}), bf16[1536,768]{1,0:T(8,128)(2,1)}) %reduce-scatter.11.cloned.1.call-update) | async-done | bytes 2359312 | tf_op jit(solution)/shard_map/reduce_scatter | solution.py:191
  556.8 304.7 %all-reduce.12 = (f32[384]{0:T(512)}, f32[384]{0:T(512)}, f32[384,2304]{1,0:T(8,128)}, f32[384]{0:T(512)}, f32[384]{0:T(512)}, /*index=5*/f32[384,768]{1,0:T(8,1...) all-reduce(f32[384]{0:T(512)S(1)} %dynamic-slice_convert_fusion.8, ...), channel_id=1, replica_groups=mesh['rep'=16,'shard'=2] {'rep'}, use_global_device_ids=true, to_apply=%region_13.14 | all-reduce | flops 3543552 | bytes 21270528 | tf_op jit(solution)/shard_map/psum | solution.py:294
  (184 shorter events, 108.7 us)
Async XLA Ops:
  7.2 53.9 %all-gather.14.cloned.1.call-start = ((), (), s32[]{:S(2)}) async-start(), calls=%async_computation.4 | async-start | bytes 5308416 | tf_op jit(solution)/shard_map/all_gather | solution.py:85
  7.9 111.8 %all-gather.16.cloned.1.call-start = ((), (), s32[]{:S(2)}) async-start(), calls=%async_computation.5 | async-start | bytes 1769472 | tf_op jit(solution)/shard_map/all_gather | solution.py:88
  8.7 141.0 %all-gather.18.cloned.1.call-start = ((), (), s32[]{:S(2)}) async-start(), calls=%async_computation.6 | async-start | bytes 7077888 | tf_op jit(solution)/shard_map/all_gather | solution.py:132
  9.4 204.3 %all-gather.20.cloned.1.call-start = ((), (), s32[]{:S(2)}) async-start(), calls=%async_computation.7 | async-start | bytes 7077888 | tf_op jit(solution)/shard_map/all_gather | solution.py:157
  10.0 7.1 copy-start.28
  10.0 10.4 %copy-start.29 = (bf16[384]{0:T(512)(128)(2,1)S(1)}, bf16[384]{0:T(512)(128)(2,1)}, u32[]{:S(2)}) copy-start(bf16[384]{0:T(512)(128)(2,1)} %param.19) | copy-start | bytes 2308
  10.0 14.0 %copy-start.30 = (bf16[384]{0:T(512)(128)(2,1)S(1)}, bf16[384]{0:T(512)(128)(2,1)}, u32[]{:S(2)}) copy-start(bf16[384]{0:T(512)(128)(2,1)} %param.20) | copy-start | bytes 2308
  10.0 17.9 %copy-start.31 = (bf16[384]{0:T(512)(128)(2,1)S(1)}, bf16[384]{0:T(512)(128)(2,1)}, u32[]{:S(2)}) copy-start(bf16[384]{0:T(512)(128)(2,1)} %param.22) | copy-start | bytes 2308
  10.0 22.2 %copy-start.32 = (bf16[384]{0:T(512)(128)(2,1)S(1)}, bf16[384]{0:T(512)(128)(2,1)}, u32[]{:S(2)}) copy-start(bf16[384]{0:T(512)(128)(2,1)} %param.23) | copy-start | bytes 2308
  10.0 25.9 %copy-start.26 = (bf16[1536]{0:T(1024)(128)(2,1)S(1)}, bf16[1536]{0:T(1024)(128)(2,1)}, u32[]{:S(2)}) copy-start(bf16[1536]{0:T(1024)(128)(2,1)} %param.26) | copy-start | bytes 9220
  10.1 30.3 %copy-start.33 = (bf16[384]{0:T(512)(128)(2,1)S(1)}, bf16[384]{0:T(512)(128)(2,1)}, u32[]{:S(2)}) copy-start(bf16[384]{0:T(512)(128)(2,1)} %param.24) | copy-start | bytes 2308
  10.1 490.8 %reduce-scatter.7.cloned.1.call-start = ((), (), s32[]{:S(2)}) async-start(), calls=%async_computation.9 | async-start | bytes 1769472 | tf_op jit(solution)/shard_map/reduce_scatter | solution.py:272
  13.0 48.1 %copy-start.10 = (f32[985,768]{1,0:T(8,128)S(1)}, f32[985,768]{1,0:T(8,128)}, u32[]{:S(2)}) copy-start(f32[985,768]{1,0:T(8,128)} %reshape.162) | copy-start | bytes 9077764
  20.4 47.0 %copy-start.23 = (f32[768]{0:T(1024)}, f32[768]{0:T(1024)S(1)}, u32[]{:S(2)}) copy-start(f32[768]{0:T(1024)S(1)} %reshape.182) | copy-start | bytes 9220
  104.9 4.5 copy-start
  119.7 4.4 copy-start.17
  124.2 25.5 %copy-start.22 = (f32[2,1,1536]{2,1,0:T(1,128)S(1)}, f32[2,1,1536]{2,1,0:T(1,128)}, u32[]{:S(2)}) copy-start(f32[2,1,1536]{2,1,0:T(1,128)} %convert_element_type.226) | copy-start | bytes 36868
  124.2 25.5 %copy-start.25 = (f32[768]{0:T(1024)S(1)}, f32[768]{0:T(1024)}, u32[]{:S(2)}) copy-start(f32[768]{0:T(1024)} %reshape.187) | copy-start | bytes 9220
  149.7 64.1 %copy-start.16 = (bf16[985,768]{1,0:T(8,128)(2,1)S(1)}, bf16[985,768]{1,0:T(8,128)(2,1)}, u32[]{:S(2)}) copy-start(bf16[985,768]{1,0:T(8,128)(2,1)} %reshape.156) | copy-start | bytes 4538884
  213.7 11.6 %copy-start.6 = (f32[985,768]{1,0:T(8,128)S(1)}, f32[985,768]{1,0:T(8,128)}, u32[]{:S(2)}) copy-start(f32[985,768]{1,0:T(8,128)} %copy-done.5) | copy-start | bytes 9077764
  213.7 11.6 %copy-start.35 = (bf16[768,3072]{1,0:T(8,128)(2,1)S(1)}, bf16[768,3072]{1,0:T(8,128)(2,1)}, u32[]{:S(2)}) copy-start(bf16[768,3072]{1,0:T(8,128)(2,1)} %all-gather.18.cloned.1.call-done) | copy-start | bytes 14155780
  225.3 5.5 copy-start.37
  244.6 6.1 copy-start.20
  260.7 240.1 %reduce-scatter.5.cloned.1.call-start = ((), (), s32[]{:S(2)}) async-start(), calls=%async_computation.8 | async-start | bytes 5308416 | tf_op jit(solution)/shard_map/reduce_scatter | solution.py:263
  260.8 8.0 copy-start.13
  271.9 5.8 copy-start.4
  301.8 5.7 copy-start.3
  345.6 155.2 %reduce-scatter.9.cloned.1.call-start = ((), (), s32[]{:S(2)}) async-start(), calls=%async_computation.10 | async-start | bytes 7077888 | tf_op jit(solution)/shard_map/reduce_scatter | solution.py:185
  357.3 199.5 %reduce-scatter.11.cloned.1.call-start = ((), (), s32[]{:S(2)}) async-start(), calls=%async_computation.11 | async-start | bytes 7077888 | tf_op jit(solution)/shard_map/reduce_scatter | solution.py:191
  366.5 91.5 %collective-permute-start = (bf16[1,1536,768]{2,1,0:T(8,128)(2,1)}, bf16[1,1536,768]{2,1,0:T(8,128)(2,1)}, u32[]{:S(2)}, u32[]{:S(2)}) collective-permute-start(bf16[1,1536,768]{2,1,0:T(8,128)(2,1)} %bitcast.50), channel_id=1, source_target_pairs={{0,1},{1,0},{2,3},{3,2},{4,5},{5,4},{6,7},{7,6},{8,9},{9,8},{10,11... | collective-permute-start | bytes 7077896 | tf_op jit(solution)/shard_map/ppermute | solution.py:25
  466.8 9.8 %copy-start.9 = (f32[985,768]{1,0:T(8,128)S(1)}, f32[985,768]{1,0:T(8,128)}, u32[]{:S(2)}) copy-start(f32[985,768]{1,0:T(8,128)} %copy-done.8) | copy-start | bytes 9077764
  466.8 9.8 %copy-start.12 = (f32[985,768]{1,0:T(8,128)S(1)}, f32[985,768]{1,0:T(8,128)}, u32[]{:S(2)}) copy-start(f32[985,768]{1,0:T(8,128)} %reshape.162) | copy-start | bytes 9077764
  (15 other events, 37.5 us)
Sparse Core Ops, SparseCore 0:
  9.5 51.5 all-gather.13
  62.6 22.7 all-gather.15
  87.0 62.6 all-gather.17
  151.1 62.6 all-gather.19
  260.8 21.8 reduce-scatter.6
  345.8 69.4 reduce-scatter.4
  417.6 77.0 reduce-scatter.8
  496.9 59.7 reduce-scatter.10
